TPU v7x, 32 devices: a whole 2x2x4 slice. The times are simulated.
32 devices in a mesh: wide: 8 (over z, x), narrow: 4 (over y, core).
Axes of the slice: x: 2, y: 2, z: 4, core: 2. Of those that a mesh axis runs over, the one named last changes fastest.
Arguments:
- pressure: float32 [1024, 128], P(('wide', 'narrow')), may hold values from -6 to 6
- right_side: float32 [1024, 128], P(('wide', 'narrow')), may hold values from -6 to 6
- concentration: float32 [1024, 128], P(('wide', 'narrow')), may hold values from 0 to 1
- pore_volume: float32 [1024, 128], P(('wide', 'narrow')), may hold values from 0.5 to 2
- well_rate: float32 [1024, 128], P(('wide', 'narrow')), may hold values from 0.02 to 0.5
- inject_conc: float32 [1024, 128], P(('wide', 'narrow')), may hold values from 0 to 1
- transmissibility: float32 [6, 131072], P(None, ('wide', 'narrow')), may hold values from 0.1 to 1
- face_neighbor: int32 [6, 1024], P(None, ('wide', 'narrow')), may hold values from 0 to 56, as said below
- sub_matrix: bfloat16 [2048, 4, 128, 128], P(('wide', 'narrow')), as said below
- sub_columns: int32 [2048, 4], P(('wide', 'narrow')), may hold values from 0 to 63, as said below
- send_blocks: int32 [32, 4, 8], P(('wide', 'narrow')), may hold values from 0 to 31, as said below
- send_counts: int32 [32, 4], P(('wide', 'narrow')), may hold values from 1 to 8, as said below
- basis_weights: bfloat16 [8192, 4096], P(('wide', 'narrow')), may hold values from -0.09375 to 0.09375
- coarse_index: int32 [8192], P(('wide', 'narrow')), may hold values from 0 to 4095, as said below
- coarse_inverse: float32 [4096, 512], P(('wide', 'narrow')), may hold values from -0.25 to 0.25
Outputs:
- pressure_new: float32 [1024, 128], P(('wide', 'narrow'))
- concentration_new: float32 [1024, 128], P(('wide', 'narrow'))
Inputs may be any that keep to these rules, and one draw needn't show every extreme that they name: `send_blocks`: local block indices below 32. `send_counts`: between 1 and 8; the first subdomain sends 8 blocks to every neighbour and the last sends one. `sub_columns`: slot 0 of each row block names the row block itself. `face_neighbor`: each owned block's faces name owned blocks or the first received block from some neighbour. `coarse_index`: a subdomain's functions may be owned by any index of wide, and may repeat. `sub_matrix`: the diagonal of each row block's first stored block lies between 0.9 and 2.1.
All inputs are finite; a program needn't handle non-finite values.
Results may differ from a plain program's by a relative error of at most 0.00225.
The roundings to bfloat16 on the way count: a program that leaves them out, or rounds other values in their place, can miss the bound.
Values may be sent and summed in bfloat16 or wider, within the bound.
A program may use at most 64 MiB of HBM per device.

v0:
```python
import jax
import jax.numpy as jnp
from jax import lax
from jax.sharding import PartitionSpec as P

SWEEPS = 4
shift_offsets = (2, 1, -1, -2)
courant = 0.9


def from_behind(value, axis, steps):
    count = lax.axis_size(axis)
    leading, last = (max(0, -steps), min(count, count - steps))
    return lax.ppermute(value, axis, [(source, source + steps) for source in range(leading, last)])


def block_product(matrix, columns, vector_b):
    picked = vector_b[columns]
    return jnp.einsum("rkij,rkj->ri", matrix, picked, preferred_element_type=jnp.float32)


def outgoing_one(owned_rows, send_blocks, send_counts):
    slot_count = send_blocks.shape[-1]
    active = jnp.arange(slot_count)[None, :] < send_counts[0][:, None]
    picked = owned_rows[send_blocks[0]]
    return jnp.where(active[:, :, None], picked, jnp.zeros_like(picked))


def with_rims(owned_list, send_blocks, send_counts, mover):
    packed = [outgoing_one(owned_rows, send_blocks, send_counts) for owned_rows in owned_list]
    arrived = [[owned_rows] for owned_rows in owned_list]
    for position, offset in enumerate(shift_offsets):
        moved_rows = mover([sent_rows[position] for sent_rows in packed], offset)
        for target, portion in zip(arrived, moved_rows):
            target.append(portion)
    return [jnp.concatenate(target, axis=0) for target in arrived]


def local(
    pressure,
    right_side,
    concentration,
    pore_volume,
    well_rate,
    inject_conc,
    transmissibility,
    face_neighbor,
    sub_matrix,
    sub_columns,
    send_blocks,
    send_counts,
    basis_weights,
    coarse_index,
    coarse_inverse,
):
    owned_count = pressure.shape[0]
    pressure_b = pressure.astype(jnp.bfloat16)
    ext_pressure = with_rims(
        [pressure_b],
        send_blocks,
        send_counts,
        lambda members, offset: (from_behind(members[0], "wide", offset),),
    )[0]
    residual = right_side - block_product(
        sub_matrix[:owned_count], sub_columns[:owned_count], ext_pressure
    )
    residual_b = residual.astype(jnp.bfloat16)
    local_coarse = jnp.dot(
        basis_weights, residual_b.reshape(-1), preferred_element_type=jnp.float32
    )
    coarse_width = coarse_inverse.shape[1]
    wide_count = lax.axis_size("wide")
    coarse_total = coarse_width * wide_count
    ext_residual = with_rims(
        [residual_b],
        send_blocks,
        send_counts,
        lambda members, offset: (from_behind(members[0], "wide", offset),),
    )[0]
    diagonal = jnp.diagonal(sub_matrix[:, 0], axis1=1, axis2=2).astype(jnp.float32)
    target_rows = ext_residual.astype(jnp.float32)
    update = jnp.zeros(target_rows.shape, jnp.float32)
    for turn_index in range(SWEEPS):
        update = (
            update
            + (target_rows - block_product(sub_matrix, sub_columns, update.astype(jnp.bfloat16)))
            / diagonal
        )
    partial_value = jnp.zeros((coarse_total,), jnp.float32).at[coarse_index].add(local_coarse)
    summed = lax.psum(partial_value, ("wide", "narrow"))
    owner_block = lax.dynamic_slice_in_dim(
        summed, lax.axis_index("wide") * coarse_width, coarse_width
    )
    block_inverse = lax.all_gather(coarse_inverse, "narrow", axis=0, tiled=True)
    owner_values = jnp.dot(block_inverse, owner_block, precision=lax.Precision.HIGHEST)
    coarse_values = lax.all_gather(owner_values, "wide", axis=0, tiled=True)
    picked_coarse = coarse_values.astype(jnp.bfloat16)[coarse_index]
    correction = jnp.dot(picked_coarse, basis_weights, preferred_element_type=jnp.float32)
    pressure_next = pressure + update[:owned_count] + correction.reshape(owned_count, -1)
    ext_next, ext_conc = with_rims(
        [pressure_next, concentration],
        send_blocks,
        send_counts,
        lambda members, offset: from_behind((members[0], members[1]), "wide", offset),
    )
    face_count = face_neighbor.shape[0]
    near_pressure = ext_next[face_neighbor].reshape(face_count, -1)
    near_conc = ext_conc[face_neighbor].reshape(face_count, -1)
    own_pressure = pressure_next.reshape(1, -1)
    conc_flat = concentration.reshape(-1)
    face_flux = transmissibility * (own_pressure - near_pressure)
    outward = jnp.maximum(face_flux, 0.0)
    inward = jnp.minimum(face_flux, 0.0)
    advection = jnp.sum(outward * conc_flat[None, :] + inward * near_conc, axis=0)
    outflow = jnp.sum(outward, axis=0)
    volume_flat = pore_volume.reshape(-1)
    rate_flat = well_rate.reshape(-1)
    cell_rate = (outflow + rate_flat) / volume_flat
    rate_top = lax.pmax(jnp.max(cell_rate), ("wide", "narrow"))
    time_step = courant / rate_top
    conc_next = conc_flat + time_step / volume_flat * (
        rate_flat * (inject_conc.reshape(-1) - conc_flat) - advection
    )
    return (pressure_next, conc_next.reshape(owned_count, -1))


def solution(mesh):
    return jax.shard_map(
        local,
        mesh=mesh,
        in_specs=(
            P(("wide", "narrow"), None),
            P(("wide", "narrow"), None),
            P(("wide", "narrow"), None),
            P(("wide", "narrow"), None),
            P(("wide", "narrow"), None),
            P(("wide", "narrow"), None),
            P(None, ("wide", "narrow")),
            P(None, ("wide", "narrow")),
            P(("wide", "narrow"), None, None, None),
            P(("wide", "narrow"), None),
            P(("wide", "narrow"), None, None),
            P(("wide", "narrow"), None),
            P(("wide", "narrow"), None),
            P(("wide", "narrow")),
            P(("wide", "narrow"), None),
        ),
        out_specs=(P(("wide", "narrow"), None), P(("wide", "narrow"), None)),
        check_vma=False,
    )
```

profile of v0, /device:TPU:0, one launch (start us, length us, event | category | flops | bytes accessed | tf_op | source)
XLA Modules:
  0.0 232.3 jit_solution(17184199817668447989)
XLA Ops:
  10.3 4.9 %collective-permute-start = (bf16[8,128]{1,0:T(8,128)(2,1)S(1)}, bf16[8,128]{1,0:T(8,128)(2,1)S(1)}, u32[]{:S(2)}, u32[]{:S(2)}) collective-permute-start(bf16[8,128]{1,0:T(8,128)(2,1)S(1)} %get-tuple-element.29), channel_id=1, source_target_pairs={{0,8},{4,12},{8,16},{12,20},{16,24},{20,28},{1,9},{5,13},{9,17},{1... | collective-permute-start | bytes 6152 | tf_op jit(solution)/shard_map/ppermute | solution.py:14
  15.2 3.4 %collective-permute-start.1 = (bf16[8,128]{1,0:T(8,128)(2,1)S(1)}, bf16[8,128]{1,0:T(8,128)(2,1)S(1)}, u32[]{:S(2)}, u32[]{:S(2)}) collective-permute-start(bf16[8,128]{1,0:T(8,128)(2,1)S(1)} %get-tuple-element.28), channel_id=1, source_target_pairs={{0,4},{4,8},{8,12},{12,16},{16,20},{20,24},{24,28},{1,5},{5,9},{9,... | collective-permute-start | bytes 6152 | tf_op jit(solution)/shard_map/ppermute | solution.py:14
  23.5 3.2 %slice.70 = bf16[64,1,128,128]{3,2,1,0:T(8,128)(2,1)} slice(bf16[64,4,128,128]{3,2,1,0:T(8,128)(2,1)} %param.23), slice={[0:64], [0:1], [0:128], [0:128]} | slice | bytes 4194304 | tf_op jit(solution)/shard_map/slice | solution.py:80
  26.7 5.3 %copy.38 = bf16[64,1,128,128]{0,3,2,1:T(8,128)(2,1)} copy(bf16[64,1,128,128]{3,2,1,0:T(8,128)(2,1)} %slice.70) | data formatting | bytes 4194304
  32.1 1.9 gather_fusion.4
  35.2 5.7 %fusion.8 = f32[64,1,128,1]{2,1,3,0:T(1,128)S(1)} fusion(bf16[64,4,128,128]{3,2,1,0:T(8,128)(2,1)} %param.23, bf16[64,4,128,1]{2,1,0,3:T(4,128)(2,1)S(1)} %bitcast.134), kind=kOutput, calls=%fused_computation.23 | convolution fusion | flops 8388608 | bytes 8486912 | tf_op jit(solution)/shard_map/rkij,rkj->ri/dot_general | solution.py:19
  42.4 3.4 %fusion = f32[32,1,128,1]{2,1,3,0:T(1,128)S(1)} fusion(bf16[64,4,128,128]{3,2,1,0:T(8,128)(2,1)} %param.23, bf16[32,4,128,1]{2,1,0,3:T(4,128)(2,1)S(1)} %bitcast.143), kind=kOutput, calls=%fused_computation.14 | convolution fusion | flops 4194304 | bytes 4243456 | tf_op jit(solution)/shard_map/rkij,rkj->ri/dot_general | solution.py:19
  46.5 6.3 %collective-permute-start.4 = (bf16[8,128]{1,0:T(8,128)(2,1)S(1)}, bf16[8,128]{1,0:T(8,128)(2,1)S(1)}, u32[]{:S(2)}, u32[]{:S(2)}) collective-permute-start(bf16[8,128]{1,0:T(8,128)(2,1)S(1)} %get-tuple-element.25), channel_id=1, source_target_pairs={{0,8},{4,12},{8,16},{12,20},{16,24},{20,28},{1,9},{5,13},{9,17},{1... | collective-permute-start | bytes 6152 | tf_op jit(solution)/shard_map/ppermute | solution.py:14
  53.5 2.0 scatter_custom_fusion
  55.4 40.0 %psum.7 = f32[4096]{0:T(1024)S(1)} all-reduce(f32[4096]{0:T(1024)S(1)} %scatter_custom_fusion), channel_id=1, replica_groups=mesh['wide'=8,'narrow'=4] {'wide','narrow'}, use_global_device_ids=true, to_apply=%region_1.2 | all-reduce | flops 4096 | bytes 32768 | tf_op jit(solution)/shard_map/psum | solution.py:90
  95.4 4.2 %collective-permute-start.5 = (bf16[8,128]{1,0:T(8,128)(2,1)S(1)}, bf16[8,128]{1,0:T(8,128)(2,1)S(1)}, u32[]{:S(2)}, u32[]{:S(2)}) collective-permute-start(bf16[8,128]{1,0:T(8,128)(2,1)S(1)} %get-tuple-element.24), channel_id=1, source_target_pairs={{0,4},{4,8},{8,12},{12,16},{16,20},{20,24},{24,28},{1,5},{5,9},{9,... | collective-permute-start | bytes 6152 | tf_op jit(solution)/shard_map/ppermute | solution.py:14
  102.5 2.6 %collective-permute-done.6 = bf16[8,128]{1,0:T(8,128)(2,1)S(1)} collective-permute-done((bf16[8,128]{1,0:T(8,128)(2,1)S(1)}, bf16[8,128]{1,0:T(8,128)(2,1)S(1)}, u32[]{:S(2)}, u32[]{:S(2)}) %collective-permute-start.6) | collective-permute-done | bytes 2080 | tf_op jit(solution)/shard_map/ppermute | solution.py:14
  107.4 5.6 %fusion.6 = f32[64,1,128,1]{2,1,3,0:T(1,128)S(1)} fusion(bf16[64,4,128,128]{3,2,1,0:T(8,128)(2,1)} %param.23, bf16[64,4,128,1]{2,1,0,3:T(4,128)(2,1)S(1)} %bitcast.135), kind=kOutput, calls=%fused_computation.21 | convolution fusion | flops 8388608 | bytes 8486912 | tf_op jit(solution)/shard_map/rkij,rkj->ri/dot_general | solution.py:19
  113.9 5.6 %fusion.4 = f32[64,1,128,1]{2,1,3,0:T(1,128)S(1)} fusion(bf16[64,4,128,128]{3,2,1,0:T(8,128)(2,1)} %param.23, bf16[64,4,128,1]{2,1,0,3:T(4,128)(2,1)S(1)} %bitcast.136), kind=kOutput, calls=%fused_computation.19 | convolution fusion | flops 8388608 | bytes 8486912 | tf_op jit(solution)/shard_map/rkij,rkj->ri/dot_general | solution.py:19
  120.5 5.6 %fusion.2 = f32[64,1,128,1]{2,1,3,0:T(1,128)S(1)} fusion(bf16[64,4,128,128]{3,2,1,0:T(8,128)(2,1)} %param.23, bf16[64,4,128,1]{2,1,0,3:T(4,128)(2,1)S(1)} %bitcast.133), kind=kOutput, calls=%fused_computation.17 | convolution fusion | flops 8388608 | bytes 8486912 | tf_op jit(solution)/shard_map/rkij,rkj->ri/dot_general | solution.py:19
  126.1 2.2 convolution_bitcast_fusion
  128.3 26.0 %all-gather = bf16[8,1,512]{2,1,0:T(2,128)(2,1)S(1)} all-gather(bf16[1,1,512]{2,1,0:T(2,128)(2,1)S(1)} %convolution_bitcast_fusion), channel_id=1, replica_groups=mesh['wide'=8,'narrow'=4] {'wide'}, dimensions={0}, use_global_device_ids=true | all-gather | bytes 9216 | tf_op jit(solution)/shard_map/all_gather | solution.py:96
  154.4 1.9 gather_fusion.8
  157.4 2.1 collective-permute-start.8
  163.9 6.5 %collective-permute-start.12 = (f32[8,128]{1,0:T(8,128)S(1)}, f32[8,128]{1,0:T(8,128)S(1)}, u32[]{:S(2)}, u32[]{:S(2)}) collective-permute-start(f32[8,128]{1,0:T(8,128)S(1)} %get-tuple-element.17), channel_id=1, source_target_pairs={{0,8},{4,12},{8,16},{12,20},{16,24},{20,28},{1,9},{5,13},{9,17},{1... | collective-permute-start | bytes 12296 | tf_op jit(solution)/shard_map/ppermute | solution.py:14
  170.4 2.6 %collective-permute-start.13 = (f32[8,128]{1,0:T(8,128)S(1)}, f32[8,128]{1,0:T(8,128)S(1)}, u32[]{:S(2)}, u32[]{:S(2)}) collective-permute-start(f32[8,128]{1,0:T(8,128)S(1)} %get-tuple-element.16), channel_id=1, source_target_pairs={{0,4},{4,8},{8,12},{12,16},{16,20},{20,24},{24,28},{1,5},{5,9},{9,... | collective-permute-start | bytes 12296 | tf_op jit(solution)/shard_map/ppermute | solution.py:14
  175.8 3.5 %collective-permute-done.14 = f32[8,128]{1,0:T(8,128)S(1)} collective-permute-done((f32[8,128]{1,0:T(8,128)S(1)}, f32[8,128]{1,0:T(8,128)S(1)}, u32[]{:S(2)}, u32[]{:S(2)}) %collective-permute-start.14) | collective-permute-done | bytes 4128 | tf_op jit(solution)/shard_map/ppermute | solution.py:14
  180.0 2.7 %collective-permute-done.15 = f32[8,128]{1,0:T(8,128)S(1)} collective-permute-done((f32[8,128]{1,0:T(8,128)S(1)}, f32[8,128]{1,0:T(8,128)S(1)}, u32[]{:S(2)}, u32[]{:S(2)}) %collective-permute-start.15) | collective-permute-done | bytes 4128 | tf_op jit(solution)/shard_map/ppermute | solution.py:14
  184.2 39.9 %pmax.7 = f32[]{:T(128)} all-reduce(f32[]{:T(128)} %fusion.16), channel_id=1, replica_groups=mesh['wide'=8,'narrow'=4] {'wide','narrow'}, use_global_device_ids=true, to_apply=%region_4.5 | all-reduce | flops 1 | bytes 8 | tf_op jit(solution)/shard_map/pmax | solution.py:119
  (120 shorter events, 29.7 us)
Async XLA Ops:
  7.2 45.6 %copy-start = (bf16[256,4096]{1,0:T(8,128)(2,1)S(1)}, bf16[256,4096]{1,0:T(8,128)(2,1)}, u32[]{:S(2)}) copy-start(bf16[256,4096]{1,0:T(8,128)(2,1)} %param.27) | copy-start | bytes 6291460
  7.2 118.9 %all-gather.3.cloned.1.call-start = ((), (), s32[]{:S(2)}) async-start(), calls=%async_computation | async-start | bytes 1310720 | tf_op jit(solution)/shard_map/all_gather | solution.py:94
  10.3 31.3 %collective-permute-start = (bf16[8,128]{1,0:T(8,128)(2,1)S(1)}, bf16[8,128]{1,0:T(8,128)(2,1)S(1)}, u32[]{:S(2)}, u32[]{:S(2)}) collective-permute-start(bf16[8,128]{1,0:T(8,128)(2,1)S(1)} %get-tuple-element.29), channel_id=1, source_target_pairs={{0,8},{4,12},{8,16},{12,20},{16,24},{20,28},{1,9},{5,13},{9,17},{1... | collective-permute-start | bytes 6152 | tf_op jit(solution)/shard_map/ppermute | solution.py:14
  15.2 26.4 %collective-permute-start.1 = (bf16[8,128]{1,0:T(8,128)(2,1)S(1)}, bf16[8,128]{1,0:T(8,128)(2,1)S(1)}, u32[]{:S(2)}, u32[]{:S(2)}) collective-permute-start(bf16[8,128]{1,0:T(8,128)(2,1)S(1)} %get-tuple-element.28), channel_id=1, source_target_pairs={{0,4},{4,8},{8,12},{12,16},{16,20},{20,24},{24,28},{1,5},{5,9},{9,... | collective-permute-start | bytes 6152 | tf_op jit(solution)/shard_map/ppermute | solution.py:14
  18.6 23.0 %collective-permute-start.2 = (bf16[8,128]{1,0:T(8,128)(2,1)S(1)}, bf16[8,128]{1,0:T(8,128)(2,1)S(1)}, u32[]{:S(2)}, u32[]{:S(2)}) collective-permute-start(bf16[8,128]{1,0:T(8,128)(2,1)S(1)} %get-tuple-element.27), channel_id=1, source_target_pairs={{4,0},{8,4},{12,8},{16,12},{20,16},{24,20},{28,24},{5,1},{9,5},{13... | collective-permute-start | bytes 6152 | tf_op jit(solution)/shard_map/ppermute | solution.py:14
  19.9 21.8 %collective-permute-start.3 = (bf16[8,128]{1,0:T(8,128)(2,1)S(1)}, bf16[8,128]{1,0:T(8,128)(2,1)S(1)}, u32[]{:S(2)}, u32[]{:S(2)}) collective-permute-start(bf16[8,128]{1,0:T(8,128)(2,1)S(1)} %get-tuple-element.26), channel_id=1, source_target_pairs={{8,0},{12,4},{16,8},{20,12},{24,16},{28,20},{9,1},{13,5},{17,9},{2... | collective-permute-start | bytes 6152 | tf_op jit(solution)/shard_map/ppermute | solution.py:14
  46.5 56.0 %collective-permute-start.4 = (bf16[8,128]{1,0:T(8,128)(2,1)S(1)}, bf16[8,128]{1,0:T(8,128)(2,1)S(1)}, u32[]{:S(2)}, u32[]{:S(2)}) collective-permute-start(bf16[8,128]{1,0:T(8,128)(2,1)S(1)} %get-tuple-element.25), channel_id=1, source_target_pairs={{0,8},{4,12},{8,16},{12,20},{16,24},{20,28},{1,9},{5,13},{9,17},{1... | collective-permute-start | bytes 6152 | tf_op jit(solution)/shard_map/ppermute | solution.py:14
  95.4 7.1 %collective-permute-start.5 = (bf16[8,128]{1,0:T(8,128)(2,1)S(1)}, bf16[8,128]{1,0:T(8,128)(2,1)S(1)}, u32[]{:S(2)}, u32[]{:S(2)}) collective-permute-start(bf16[8,128]{1,0:T(8,128)(2,1)S(1)} %get-tuple-element.24), channel_id=1, source_target_pairs={{0,4},{4,8},{8,12},{12,16},{16,20},{20,24},{24,28},{1,5},{5,9},{9,... | collective-permute-start | bytes 6152 | tf_op jit(solution)/shard_map/ppermute | solution.py:14
  99.6 5.5 %collective-permute-start.6 = (bf16[8,128]{1,0:T(8,128)(2,1)S(1)}, bf16[8,128]{1,0:T(8,128)(2,1)S(1)}, u32[]{:S(2)}, u32[]{:S(2)}) collective-permute-start(bf16[8,128]{1,0:T(8,128)(2,1)S(1)} %get-tuple-element.23), channel_id=1, source_target_pairs={{4,0},{8,4},{12,8},{16,12},{20,16},{24,20},{28,24},{5,1},{9,5},{13... | collective-permute-start | bytes 6152 | tf_op jit(solution)/shard_map/ppermute | solution.py:14
  100.9 5.6 %collective-permute-start.7 = (bf16[8,128]{1,0:T(8,128)(2,1)S(1)}, bf16[8,128]{1,0:T(8,128)(2,1)S(1)}, u32[]{:S(2)}, u32[]{:S(2)}) collective-permute-start(bf16[8,128]{1,0:T(8,128)(2,1)S(1)} %get-tuple-element.22), channel_id=1, source_target_pairs={{8,0},{12,4},{16,8},{20,12},{24,16},{28,20},{9,1},{13,5},{17,9},{2... | collective-permute-start | bytes 6152 | tf_op jit(solution)/shard_map/ppermute | solution.py:14
  119.5 37.2 %copy-start.6 = (f32[32,128]{1,0:T(8,128)S(1)}, f32[32,128]{1,0:T(8,128)}, u32[]{:S(2)}) copy-start(f32[32,128]{1,0:T(8,128)} %param.15) | copy-start | bytes 49156
  119.5 63.9 %copy-start.3 = (f32[6,4096]{1,0:T(8,128)S(1)}, f32[6,4096]{1,0:T(8,128)}, u32[]{:S(2)}) copy-start(f32[6,4096]{1,0:T(8,128)} %param.21) | copy-start | bytes 294916
  119.5 64.0 %copy-start.4 = (f32[32,128]{1,0:T(8,128)S(1)}, f32[32,128]{1,0:T(8,128)}, u32[]{:S(2)}) copy-start(f32[32,128]{1,0:T(8,128)} %param.19) | copy-start | bytes 49156
  119.5 64.0 %copy-start.5 = (f32[32,128]{1,0:T(8,128)S(1)}, f32[32,128]{1,0:T(8,128)}, u32[]{:S(2)}) copy-start(f32[32,128]{1,0:T(8,128)} %param.18) | copy-start | bytes 49156
  119.6 105.2 %copy-start.8 = (f32[32,128]{1,0:T(8,128)S(1)}, f32[32,128]{1,0:T(8,128)}, u32[]{:S(2)}) copy-start(f32[32,128]{1,0:T(8,128)} %param.20) | copy-start | bytes 49156
  156.7 68.7 %copy-start.2 = (f32[32,128]{1,0:T(8,128)}, f32[32,128]{1,0:T(8,128)S(1)}, u32[]{:S(2)}) copy-start(f32[32,128]{1,0:T(8,128)S(1)} %get-tuple-element.5) | copy-start | bytes 49156
  157.4 13.0 %collective-permute-start.8 = (f32[8,128]{1,0:T(8,128)S(1)}, f32[8,128]{1,0:T(8,128)S(1)}, u32[]{:S(2)}, u32[]{:S(2)}) collective-permute-start(f32[8,128]{1,0:T(8,128)S(1)} %get-tuple-element.21), channel_id=1, source_target_pairs={{0,8},{4,12},{8,16},{12,20},{16,24},{20,28},{1,9},{5,13},{9,17},{1... | collective-permute-start | bytes 12296 | tf_op jit(solution)/shard_map/ppermute | solution.py:14
  159.5 13.5 %collective-permute-start.9 = (f32[8,128]{1,0:T(8,128)S(1)}, f32[8,128]{1,0:T(8,128)S(1)}, u32[]{:S(2)}, u32[]{:S(2)}) collective-permute-start(f32[8,128]{1,0:T(8,128)S(1)} %get-tuple-element.20), channel_id=1, source_target_pairs={{0,4},{4,8},{8,12},{12,16},{16,20},{20,24},{24,28},{1,5},{5,9},{9,... | collective-permute-start | bytes 12296 | tf_op jit(solution)/shard_map/ppermute | solution.py:14
  161.3 13.1 %collective-permute-start.10 = (f32[8,128]{1,0:T(8,128)S(1)}, f32[8,128]{1,0:T(8,128)S(1)}, u32[]{:S(2)}, u32[]{:S(2)}) collective-permute-start(f32[8,128]{1,0:T(8,128)S(1)} %get-tuple-element.19), channel_id=1, source_target_pairs={{4,0},{8,4},{12,8},{16,12},{20,16},{24,20},{28,24},{5,1},{9,5},{13... | collective-permute-start | bytes 12296 | tf_op jit(solution)/shard_map/ppermute | solution.py:14
  162.6 13.1 %collective-permute-start.11 = (f32[8,128]{1,0:T(8,128)S(1)}, f32[8,128]{1,0:T(8,128)S(1)}, u32[]{:S(2)}, u32[]{:S(2)}) collective-permute-start(f32[8,128]{1,0:T(8,128)S(1)} %get-tuple-element.18), channel_id=1, source_target_pairs={{8,0},{12,4},{16,8},{20,12},{24,16},{28,20},{9,1},{13,5},{17,9},{2... | collective-permute-start | bytes 12296 | tf_op jit(solution)/shard_map/ppermute | solution.py:14
  163.9 11.8 %collective-permute-start.12 = (f32[8,128]{1,0:T(8,128)S(1)}, f32[8,128]{1,0:T(8,128)S(1)}, u32[]{:S(2)}, u32[]{:S(2)}) collective-permute-start(f32[8,128]{1,0:T(8,128)S(1)} %get-tuple-element.17), channel_id=1, source_target_pairs={{0,8},{4,12},{8,16},{12,20},{16,24},{20,28},{1,9},{5,13},{9,17},{1... | collective-permute-start | bytes 12296 | tf_op jit(solution)/shard_map/ppermute | solution.py:14
  170.4 5.3 %collective-permute-start.13 = (f32[8,128]{1,0:T(8,128)S(1)}, f32[8,128]{1,0:T(8,128)S(1)}, u32[]{:S(2)}, u32[]{:S(2)}) collective-permute-start(f32[8,128]{1,0:T(8,128)S(1)} %get-tuple-element.16), channel_id=1, source_target_pairs={{0,4},{4,8},{8,12},{12,16},{16,20},{20,24},{24,28},{1,5},{5,9},{9,... | collective-permute-start | bytes 12296 | tf_op jit(solution)/shard_map/ppermute | solution.py:14
  173.1 6.2 %collective-permute-start.14 = (f32[8,128]{1,0:T(8,128)S(1)}, f32[8,128]{1,0:T(8,128)S(1)}, u32[]{:S(2)}, u32[]{:S(2)}) collective-permute-start(f32[8,128]{1,0:T(8,128)S(1)} %get-tuple-element.15), channel_id=1, source_target_pairs={{4,0},{8,4},{12,8},{16,12},{20,16},{24,20},{28,24},{5,1},{9,5},{13... | collective-permute-start | bytes 12296 | tf_op jit(solution)/shard_map/ppermute | solution.py:14
  174.4 8.3 %collective-permute-start.15 = (f32[8,128]{1,0:T(8,128)S(1)}, f32[8,128]{1,0:T(8,128)S(1)}, u32[]{:S(2)}, u32[]{:S(2)}) collective-permute-start(f32[8,128]{1,0:T(8,128)S(1)} %get-tuple-element.14), channel_id=1, source_target_pairs={{8,0},{12,4},{16,8},{20,12},{24,16},{28,20},{9,1},{13,5},{17,9},{2... | collective-permute-start | bytes 12296 | tf_op jit(solution)/shard_map/ppermute | solution.py:14
  (3 other events, 42.1 us)
Sparse Core Ops, SparseCore 0:
  21.3 20.1 all-gather.2
where the time goes:
time: 233 us; the launch traced here: 232 us
  blocking collectives  106 us (45%)
  starting transfers between devices  42.4 us (18%)
  matrix products  29.2 us (13%)
  local copies, waits for them, and re-layouts  21.3 us (9%)
  between operations  15.3 us (7%)
  waiting for transfers between devices  10.2 us (4%)
  other arithmetic  8.01 us (3%)
    ppermute x16, starting transfers between devices, from_behind(): lax.ppermute(value, axis, [(source, source + steps) for source in range(l...  42.3 us
    psum x1, blocking collectives, local(): summed = lax.psum(partial_value, ('wide', 'narrow'))  40 us
    pmax x1, blocking collectives, local(): rate_top = lax.pmax(jnp.max(cell_rate), ('wide', 'narrow'))  39.9 us
    all_gather x1, blocking collectives, local(): coarse_values = lax.all_gather(owner_values, 'wide', axis=0, tiled=True)  26 us
    dot_general x5, matrix products, block_product(): jnp.einsum('rkij,rkj->ri', matrix, picked, preferred_element_type=jnp.flo...  26 us
    ppermute x16, waiting for transfers between devices, from_behind(): lax.ppermute(value, axis, [(source, source + steps) for source in range(l...  10.2 us
    unnamed x35, local copies, waits for them, and re-layouts  5.47 us
  transfers between devices with their start and end apart: 17, of which 4 were waited for; matrix products, arithmetic and copies ran while one was open for 21% of the time, Pallas kernels for 0%

commit v1 on v0

--- a/solution.py
+++ b/solution.py
@@ -93,7 +93,12 @@
     )
     block_inverse = lax.all_gather(coarse_inverse, "narrow", axis=0, tiled=True)
     owner_values = jnp.dot(block_inverse, owner_block, precision=lax.Precision.HIGHEST)
-    coarse_values = lax.all_gather(owner_values, "wide", axis=0, tiled=True)
+    ring = [owner_values]
+    for hop in range(7):
+        ring.append(lax.ppermute(ring[-1], "wide", [(dev, (dev + 1) % 8) for dev in range(8)]))
+    coarse_values = jnp.roll(
+        jnp.concatenate(ring[::-1], axis=0), (lax.axis_index("wide") + 1) * ring[0].shape[0], axis=0
+    )
     picked_coarse = coarse_values.astype(jnp.bfloat16)[coarse_index]
     correction = jnp.dot(picked_coarse, basis_weights, preferred_element_type=jnp.float32)
     pressure_next = pressure + update[:owned_count] + correction.reshape(owned_count, -1)

time: 233 us -> 232 us (level)
  blocking collectives: 106 us -> 81.1 us
  waiting for transfers between devices: 10.2 us -> 32.8 us
    all_gather x1 -> x0, blocking collectives: 26 us -> none  [local(): coarse_values = lax.all_gather(owner_values, 'wide', axis=0, tiled=True)]
    ppermute x0 -> x7, waiting for transfers between devices: none -> 23.4 us  [local(): lax.ppermute(ring[-1], 'wide', [(dev, (dev + 1) % 8) for dev in range(8)])]
    unnamed x35 -> x49, local copies, waits for them, and re-layouts: 5.47 us -> 5.52 us
  transfers between devices with their start and end apart: 17 -> 24, of which waited for: 4 -> 10; matrix products, arithmetic and copies ran while one was open for 21% -> 22% of each run, Pallas kernels for 0% -> 0%
where the time goes in v1:
time: 232 us; the launch traced here: 231 us
  blocking collectives  81.1 us (35%)
  starting transfers between devices  43.2 us (19%)
  waiting for transfers between devices  32.8 us (14%)
  matrix products  29.2 us (13%)
  local copies, waits for them, and re-layouts  21.4 us (9%)
  between operations  15.4 us (7%)
  other arithmetic  8 us (3%)
    ppermute x16, starting transfers between devices, from_behind(): lax.ppermute(value, axis, [(source, source + steps) for source in range(l...  42.2 us
    pmax x1, blocking collectives, local(): rate_top = lax.pmax(jnp.max(cell_rate), ('wide', 'narrow'))  41.1 us
    psum x1, blocking collectives, local(): summed = lax.psum(partial_value, ('wide', 'narrow'))  40 us
    dot_general x5, matrix products, block_product(): jnp.einsum('rkij,rkj->ri', matrix, picked, preferred_element_type=jnp.flo...  26 us
    ppermute x7, waiting for transfers between devices, local(): lax.ppermute(ring[-1], 'wide', [(dev, (dev + 1) % 8) for dev in range(8)])  23.4 us
    ppermute x16, waiting for transfers between devices, from_behind(): lax.ppermute(value, axis, [(source, source + steps) for source in range(l...  9.34 us
    unnamed x49, local copies, waits for them, and re-layouts  5.52 us
  transfers between devices with their start and end apart: 24, of which 10 were waited for; matrix products, arithmetic and copies ran while one was open for 22% of the time, Pallas kernels for 0%

profile of v1, /device:TPU:0, one launch (start us, length us, event | category | flops | bytes accessed | tf_op | source)
XLA Modules:
  0.0 231.0 jit_solution(11026153504620166475)
XLA Ops:
  10.3 4.9 %collective-permute-start = (bf16[8,128]{1,0:T(8,128)(2,1)S(1)}, bf16[8,128]{1,0:T(8,128)(2,1)S(1)}, u32[]{:S(2)}, u32[]{:S(2)}) collective-permute-start(bf16[8,128]{1,0:T(8,128)(2,1)S(1)} %get-tuple-element.29), channel_id=1, source_target_pairs={{0,8},{4,12},{8,16},{12,20},{16,24},{20,28},{1,9},{5,13},{9,17},{1... | collective-permute-start | bytes 6152 | tf_op jit(solution)/shard_map/ppermute | solution.py:14
  15.2 3.4 %collective-permute-start.1 = (bf16[8,128]{1,0:T(8,128)(2,1)S(1)}, bf16[8,128]{1,0:T(8,128)(2,1)S(1)}, u32[]{:S(2)}, u32[]{:S(2)}) collective-permute-start(bf16[8,128]{1,0:T(8,128)(2,1)S(1)} %get-tuple-element.28), channel_id=1, source_target_pairs={{0,4},{4,8},{8,12},{12,16},{16,20},{20,24},{24,28},{1,5},{5,9},{9,... | collective-permute-start | bytes 6152 | tf_op jit(solution)/shard_map/ppermute | solution.py:14
  23.5 3.2 %slice.70 = bf16[64,1,128,128]{3,2,1,0:T(8,128)(2,1)} slice(bf16[64,4,128,128]{3,2,1,0:T(8,128)(2,1)} %param.23), slice={[0:64], [0:1], [0:128], [0:128]} | slice | bytes 4194304 | tf_op jit(solution)/shard_map/slice | solution.py:80
  26.7 5.3 %copy.34 = bf16[64,1,128,128]{0,3,2,1:T(8,128)(2,1)} copy(bf16[64,1,128,128]{3,2,1,0:T(8,128)(2,1)} %slice.70) | data formatting | bytes 4194304
  35.2 5.7 %fusion.8 = f32[64,1,128,1]{2,1,3,0:T(1,128)S(1)} fusion(bf16[64,4,128,128]{3,2,1,0:T(8,128)(2,1)} %param.23, bf16[64,4,128,1]{2,1,0,3:T(4,128)(2,1)S(1)} %bitcast.130), kind=kOutput, calls=%fused_computation.22 | convolution fusion | flops 8388608 | bytes 8486912 | tf_op jit(solution)/shard_map/rkij,rkj->ri/dot_general | solution.py:19
  42.4 3.4 %fusion = f32[32,1,128,1]{2,1,3,0:T(1,128)S(1)} fusion(bf16[64,4,128,128]{3,2,1,0:T(8,128)(2,1)} %param.23, bf16[32,4,128,1]{2,1,0,3:T(4,128)(2,1)S(1)} %bitcast.137), kind=kOutput, calls=%fused_computation.14 | convolution fusion | flops 4194304 | bytes 4243456 | tf_op jit(solution)/shard_map/rkij,rkj->ri/dot_general | solution.py:19
  46.5 6.3 %collective-permute-start.4 = (bf16[8,128]{1,0:T(8,128)(2,1)S(1)}, bf16[8,128]{1,0:T(8,128)(2,1)S(1)}, u32[]{:S(2)}, u32[]{:S(2)}) collective-permute-start(bf16[8,128]{1,0:T(8,128)(2,1)S(1)} %get-tuple-element.25), channel_id=1, source_target_pairs={{0,8},{4,12},{8,16},{12,20},{16,24},{20,28},{1,9},{5,13},{9,17},{1... | collective-permute-start | bytes 6152 | tf_op jit(solution)/shard_map/ppermute | solution.py:14
  53.5 2.0 scatter_custom_fusion
  55.4 40.0 %psum.7 = f32[4096]{0:T(1024)S(1)} all-reduce(f32[4096]{0:T(1024)S(1)} %scatter_custom_fusion), channel_id=1, replica_groups=mesh['wide'=8,'narrow'=4] {'wide','narrow'}, use_global_device_ids=true, to_apply=%region_1.2 | all-reduce | flops 4096 | bytes 32768 | tf_op jit(solution)/shard_map/psum | solution.py:90
  95.4 4.2 %collective-permute-start.5 = (bf16[8,128]{1,0:T(8,128)(2,1)S(1)}, bf16[8,128]{1,0:T(8,128)(2,1)S(1)}, u32[]{:S(2)}, u32[]{:S(2)}) collective-permute-start(bf16[8,128]{1,0:T(8,128)(2,1)S(1)} %get-tuple-element.24), channel_id=1, source_target_pairs={{0,4},{4,8},{8,12},{12,16},{16,20},{20,24},{24,28},{1,5},{5,9},{9,... | collective-permute-start | bytes 6152 | tf_op jit(solution)/shard_map/ppermute | solution.py:14
  102.3 2.8 %collective-permute-done.6 = bf16[8,128]{1,0:T(8,128)(2,1)S(1)} collective-permute-done((bf16[8,128]{1,0:T(8,128)(2,1)S(1)}, bf16[8,128]{1,0:T(8,128)(2,1)S(1)}, u32[]{:S(2)}, u32[]{:S(2)}) %collective-permute-start.6) | collective-permute-done | bytes 2080 | tf_op jit(solution)/shard_map/ppermute | solution.py:14
  105.1 2.2 fusion.24
  108.2 5.4 %collective-permute-done.8 = f32[512]{0:T(512)S(1)} collective-permute-done((f32[512]{0:T(512)S(1)}, f32[512]{0:T(512)S(1)}, u32[]{:S(2)}, u32[]{:S(2)}) %collective-permute-start.8) | collective-permute-done | bytes 2080 | tf_op jit(solution)/shard_map/ppermute | solution.py:98
  114.5 5.4 %collective-permute-done.9 = f32[512]{0:T(512)S(1)} collective-permute-done((f32[512]{0:T(512)S(1)}, f32[512]{0:T(512)S(1)}, u32[]{:S(2)}, u32[]{:S(2)}) %collective-permute-start.9) | collective-permute-done | bytes 2080 | tf_op jit(solution)/shard_map/ppermute | solution.py:98
  119.9 5.6 %fusion.6 = f32[64,1,128,1]{2,1,3,0:T(1,128)S(1)} fusion(bf16[64,4,128,128]{3,2,1,0:T(8,128)(2,1)} %param.23, bf16[64,4,128,1]{2,1,0,3:T(4,128)(2,1)S(1)} %bitcast.128), kind=kOutput, calls=%fused_computation.20 | convolution fusion | flops 8388608 | bytes 8486912 | tf_op jit(solution)/shard_map/rkij,rkj->ri/dot_general | solution.py:19
  127.0 5.4 %collective-permute-done.11 = f32[512]{0:T(512)S(1)} collective-permute-done((f32[512]{0:T(512)S(1)}, f32[512]{0:T(512)S(1)}, u32[]{:S(2)}, u32[]{:S(2)}) %collective-permute-start.11) | collective-permute-done | bytes 2080 | tf_op jit(solution)/shard_map/ppermute | solution.py:98
  132.4 5.7 %fusion.4 = f32[64,1,128,1]{2,1,3,0:T(1,128)S(1)} fusion(bf16[64,4,128,128]{3,2,1,0:T(8,128)(2,1)} %param.23, bf16[64,4,128,1]{2,1,0,3:T(4,128)(2,1)S(1)} %bitcast.129), kind=kOutput, calls=%fused_computation.18 | convolution fusion | flops 8388608 | bytes 8486912 | tf_op jit(solution)/shard_map/rkij,rkj->ri/dot_general | solution.py:19
  139.6 5.4 %collective-permute-done.13 = f32[512]{0:T(512)S(1)} collective-permute-done((f32[512]{0:T(512)S(1)}, f32[512]{0:T(512)S(1)}, u32[]{:S(2)}, u32[]{:S(2)}) %collective-permute-start.13) | collective-permute-done | bytes 2080 | tf_op jit(solution)/shard_map/ppermute | solution.py:98
  145.0 5.6 %fusion.2 = f32[64,1,128,1]{2,1,3,0:T(1,128)S(1)} fusion(bf16[64,4,128,128]{3,2,1,0:T(8,128)(2,1)} %param.23, bf16[64,4,128,1]{2,1,0,3:T(4,128)(2,1)S(1)} %bitcast.127), kind=kOutput, calls=%fused_computation.16 | convolution fusion | flops 8388608 | bytes 8486912 | tf_op jit(solution)/shard_map/rkij,rkj->ri/dot_general | solution.py:19
  159.8 6.4 %collective-permute-start.19 = (f32[8,128]{1,0:T(8,128)S(1)}, f32[8,128]{1,0:T(8,128)S(1)}, u32[]{:S(2)}, u32[]{:S(2)}) collective-permute-start(f32[8,128]{1,0:T(8,128)S(1)} %get-tuple-element.17), channel_id=1, source_target_pairs={{0,8},{4,12},{8,16},{12,20},{16,24},{20,28},{1,9},{5,13},{9,17},{1... | collective-permute-start | bytes 12296 | tf_op jit(solution)/shard_map/ppermute | solution.py:14
  166.2 4.2 %collective-permute-start.20 = (f32[8,128]{1,0:T(8,128)S(1)}, f32[8,128]{1,0:T(8,128)S(1)}, u32[]{:S(2)}, u32[]{:S(2)}) collective-permute-start(f32[8,128]{1,0:T(8,128)S(1)} %get-tuple-element.16), channel_id=1, source_target_pairs={{0,4},{4,8},{8,12},{12,16},{16,20},{20,24},{24,28},{1,5},{5,9},{9,... | collective-permute-start | bytes 12296 | tf_op jit(solution)/shard_map/ppermute | solution.py:14
  173.1 3.8 %collective-permute-done.21 = f32[8,128]{1,0:T(8,128)S(1)} collective-permute-done((f32[8,128]{1,0:T(8,128)S(1)}, f32[8,128]{1,0:T(8,128)S(1)}, u32[]{:S(2)}, u32[]{:S(2)}) %collective-permute-start.21) | collective-permute-done | bytes 4128 | tf_op jit(solution)/shard_map/ppermute | solution.py:14
  177.6 2.7 %collective-permute-done.22 = f32[8,128]{1,0:T(8,128)S(1)} collective-permute-done((f32[8,128]{1,0:T(8,128)S(1)}, f32[8,128]{1,0:T(8,128)S(1)}, u32[]{:S(2)}, u32[]{:S(2)}) %collective-permute-start.22) | collective-permute-done | bytes 4128 | tf_op jit(solution)/shard_map/ppermute | solution.py:14
  181.8 41.1 %pmax.7 = f32[]{:T(128)} all-reduce(f32[]{:T(128)} %fusion.16), channel_id=1, replica_groups=mesh['wide'=8,'narrow'=4] {'wide','narrow'}, use_global_device_ids=true, to_apply=%region_4.5 | all-reduce | flops 1 | bytes 8 | tf_op jit(solution)/shard_map/pmax | solution.py:124
  (149 shorter events, 35.7 us)
Async XLA Ops:
  7.2 97.9 %all-gather.2.cloned.1.call-start = ((), (), s32[]{:S(2)}) async-start(), calls=%async_computation | async-start | bytes 1310720 | tf_op jit(solution)/shard_map/all_gather | solution.py:94
  10.3 31.3 %collective-permute-start = (bf16[8,128]{1,0:T(8,128)(2,1)S(1)}, bf16[8,128]{1,0:T(8,128)(2,1)S(1)}, u32[]{:S(2)}, u32[]{:S(2)}) collective-permute-start(bf16[8,128]{1,0:T(8,128)(2,1)S(1)} %get-tuple-element.29), channel_id=1, source_target_pairs={{0,8},{4,12},{8,16},{12,20},{16,24},{20,28},{1,9},{5,13},{9,17},{1... | collective-permute-start | bytes 6152 | tf_op jit(solution)/shard_map/ppermute | solution.py:14
  15.2 26.4 %collective-permute-start.1 = (bf16[8,128]{1,0:T(8,128)(2,1)S(1)}, bf16[8,128]{1,0:T(8,128)(2,1)S(1)}, u32[]{:S(2)}, u32[]{:S(2)}) collective-permute-start(bf16[8,128]{1,0:T(8,128)(2,1)S(1)} %get-tuple-element.28), channel_id=1, source_target_pairs={{0,4},{4,8},{8,12},{12,16},{16,20},{20,24},{24,28},{1,5},{5,9},{9,... | collective-permute-start | bytes 6152 | tf_op jit(solution)/shard_map/ppermute | solution.py:14
  18.6 23.0 %collective-permute-start.2 = (bf16[8,128]{1,0:T(8,128)(2,1)S(1)}, bf16[8,128]{1,0:T(8,128)(2,1)S(1)}, u32[]{:S(2)}, u32[]{:S(2)}) collective-permute-start(bf16[8,128]{1,0:T(8,128)(2,1)S(1)} %get-tuple-element.27), channel_id=1, source_target_pairs={{4,0},{8,4},{12,8},{16,12},{20,16},{24,20},{28,24},{5,1},{9,5},{13... | collective-permute-start | bytes 6152 | tf_op jit(solution)/shard_map/ppermute | solution.py:14
  19.9 21.8 %collective-permute-start.3 = (bf16[8,128]{1,0:T(8,128)(2,1)S(1)}, bf16[8,128]{1,0:T(8,128)(2,1)S(1)}, u32[]{:S(2)}, u32[]{:S(2)}) collective-permute-start(bf16[8,128]{1,0:T(8,128)(2,1)S(1)} %get-tuple-element.26), channel_id=1, source_target_pairs={{8,0},{12,4},{16,8},{20,12},{24,16},{28,20},{9,1},{13,5},{17,9},{2... | collective-permute-start | bytes 6152 | tf_op jit(solution)/shard_map/ppermute | solution.py:14
  46.5 55.8 %collective-permute-start.4 = (bf16[8,128]{1,0:T(8,128)(2,1)S(1)}, bf16[8,128]{1,0:T(8,128)(2,1)S(1)}, u32[]{:S(2)}, u32[]{:S(2)}) collective-permute-start(bf16[8,128]{1,0:T(8,128)(2,1)S(1)} %get-tuple-element.25), channel_id=1, source_target_pairs={{0,8},{4,12},{8,16},{12,20},{16,24},{20,28},{1,9},{5,13},{9,17},{1... | collective-permute-start | bytes 6152 | tf_op jit(solution)/shard_map/ppermute | solution.py:14
  95.4 6.9 %collective-permute-start.5 = (bf16[8,128]{1,0:T(8,128)(2,1)S(1)}, bf16[8,128]{1,0:T(8,128)(2,1)S(1)}, u32[]{:S(2)}, u32[]{:S(2)}) collective-permute-start(bf16[8,128]{1,0:T(8,128)(2,1)S(1)} %get-tuple-element.24), channel_id=1, source_target_pairs={{0,4},{4,8},{8,12},{12,16},{16,20},{20,24},{24,28},{1,5},{5,9},{9,... | collective-permute-start | bytes 6152 | tf_op jit(solution)/shard_map/ppermute | solution.py:14
  99.6 5.5 %collective-permute-start.6 = (bf16[8,128]{1,0:T(8,128)(2,1)S(1)}, bf16[8,128]{1,0:T(8,128)(2,1)S(1)}, u32[]{:S(2)}, u32[]{:S(2)}) collective-permute-start(bf16[8,128]{1,0:T(8,128)(2,1)S(1)} %get-tuple-element.23), channel_id=1, source_target_pairs={{4,0},{8,4},{12,8},{16,12},{20,16},{24,20},{28,24},{5,1},{9,5},{13... | collective-permute-start | bytes 6152 | tf_op jit(solution)/shard_map/ppermute | solution.py:14
  100.9 7.3 %collective-permute-start.7 = (bf16[8,128]{1,0:T(8,128)(2,1)S(1)}, bf16[8,128]{1,0:T(8,128)(2,1)S(1)}, u32[]{:S(2)}, u32[]{:S(2)}) collective-permute-start(bf16[8,128]{1,0:T(8,128)(2,1)S(1)} %get-tuple-element.22), channel_id=1, source_target_pairs={{8,0},{12,4},{16,8},{20,12},{24,16},{28,20},{9,1},{13,5},{17,9},{2... | collective-permute-start | bytes 6152 | tf_op jit(solution)/shard_map/ppermute | solution.py:14
  107.3 6.3 %collective-permute-start.8 = (f32[512]{0:T(512)S(1)}, f32[512]{0:T(512)S(1)}, u32[]{:S(2)}, u32[]{:S(2)}) collective-permute-start(f32[512]{0:T(512)S(1)} %bitcast.138), channel_id=1, source_target_pairs={{0,4},{4,8},{8,12},{12,16},{16,20},{20,24},{24,28},{28,0},{1,5},{5... | collective-permute-start | bytes 6152 | tf_op jit(solution)/shard_map/ppermute | solution.py:98
  113.6 6.3 %collective-permute-start.9 = (f32[512]{0:T(512)S(1)}, f32[512]{0:T(512)S(1)}, u32[]{:S(2)}, u32[]{:S(2)}) collective-permute-start(f32[512]{0:T(512)S(1)} %collective-permute-done.8), channel_id=1, source_target_pairs={{0,4},{4,8},{8,12},{12,16},{16,20},{20,24},{24,28},{28,0},{1,5},{5... | collective-permute-start | bytes 6152 | tf_op jit(solution)/shard_map/ppermute | solution.py:98
  119.9 6.3 %collective-permute-start.10 = (f32[512]{0:T(512)S(1)}, f32[512]{0:T(512)S(1)}, u32[]{:S(2)}, u32[]{:S(2)}) collective-permute-start(f32[512]{0:T(512)S(1)} %collective-permute-done.9), channel_id=1, source_target_pairs={{0,4},{4,8},{8,12},{12,16},{16,20},{20,24},{24,28},{28,0},{1,5},{5... | collective-permute-start | bytes 6152 | tf_op jit(solution)/shard_map/ppermute | solution.py:98
  126.1 6.3 %collective-permute-start.11 = (f32[512]{0:T(512)S(1)}, f32[512]{0:T(512)S(1)}, u32[]{:S(2)}, u32[]{:S(2)}) collective-permute-start(f32[512]{0:T(512)S(1)} %collective-permute-done.10), channel_id=1, source_target_pairs={{0,4},{4,8},{8,12},{12,16},{16,20},{20,24},{24,28},{28,0},{1,5},{5... | collective-permute-start | bytes 6152 | tf_op jit(solution)/shard_map/ppermute | solution.py:98
  132.4 6.3 %collective-permute-start.12 = (f32[512]{0:T(512)S(1)}, f32[512]{0:T(512)S(1)}, u32[]{:S(2)}, u32[]{:S(2)}) collective-permute-start(f32[512]{0:T(512)S(1)} %collective-permute-done.11), channel_id=1, source_target_pairs={{0,4},{4,8},{8,12},{12,16},{16,20},{20,24},{24,28},{28,0},{1,5},{5... | collective-permute-start | bytes 6152 | tf_op jit(solution)/shard_map/ppermute | solution.py:98
  138.7 6.3 %collective-permute-start.13 = (f32[512]{0:T(512)S(1)}, f32[512]{0:T(512)S(1)}, u32[]{:S(2)}, u32[]{:S(2)}) collective-permute-start(f32[512]{0:T(512)S(1)} %collective-permute-done.12), channel_id=1, source_target_pairs={{0,4},{4,8},{8,12},{12,16},{16,20},{20,24},{24,28},{28,0},{1,5},{5... | collective-permute-start | bytes 6152 | tf_op jit(solution)/shard_map/ppermute | solution.py:98
  145.0 6.3 %collective-permute-start.14 = (f32[512]{0:T(512)S(1)}, f32[512]{0:T(512)S(1)}, u32[]{:S(2)}, u32[]{:S(2)}) collective-permute-start(f32[512]{0:T(512)S(1)} %collective-permute-done.13), channel_id=1, source_target_pairs={{0,4},{4,8},{8,12},{12,16},{16,20},{20,24},{24,28},{28,0},{1,5},{5... | collective-permute-start | bytes 6152 | tf_op jit(solution)/shard_map/ppermute | solution.py:98
  154.6 11.6 %collective-permute-start.15 = (f32[8,128]{1,0:T(8,128)S(1)}, f32[8,128]{1,0:T(8,128)S(1)}, u32[]{:S(2)}, u32[]{:S(2)}) collective-permute-start(f32[8,128]{1,0:T(8,128)S(1)} %get-tuple-element.21), channel_id=1, source_target_pairs={{0,8},{4,12},{8,16},{12,20},{16,24},{20,28},{1,9},{5,13},{9,17},{1... | collective-permute-start | bytes 12296 | tf_op jit(solution)/shard_map/ppermute | solution.py:14
  155.9 14.5 %collective-permute-start.16 = (f32[8,128]{1,0:T(8,128)S(1)}, f32[8,128]{1,0:T(8,128)S(1)}, u32[]{:S(2)}, u32[]{:S(2)}) collective-permute-start(f32[8,128]{1,0:T(8,128)S(1)} %get-tuple-element.20), channel_id=1, source_target_pairs={{0,4},{4,8},{8,12},{12,16},{16,20},{20,24},{24,28},{1,5},{5,9},{9,... | collective-permute-start | bytes 12296 | tf_op jit(solution)/shard_map/ppermute | solution.py:14
  157.2 14.5 %collective-permute-start.17 = (f32[8,128]{1,0:T(8,128)S(1)}, f32[8,128]{1,0:T(8,128)S(1)}, u32[]{:S(2)}, u32[]{:S(2)}) collective-permute-start(f32[8,128]{1,0:T(8,128)S(1)} %get-tuple-element.19), channel_id=1, source_target_pairs={{4,0},{8,4},{12,8},{16,12},{20,16},{24,20},{28,24},{5,1},{9,5},{13... | collective-permute-start | bytes 12296 | tf_op jit(solution)/shard_map/ppermute | solution.py:14
  158.5 14.5 %collective-permute-start.18 = (f32[8,128]{1,0:T(8,128)S(1)}, f32[8,128]{1,0:T(8,128)S(1)}, u32[]{:S(2)}, u32[]{:S(2)}) collective-permute-start(f32[8,128]{1,0:T(8,128)S(1)} %get-tuple-element.18), channel_id=1, source_target_pairs={{8,0},{12,4},{16,8},{20,12},{24,16},{28,20},{9,1},{13,5},{17,9},{2... | collective-permute-start | bytes 12296 | tf_op jit(solution)/shard_map/ppermute | solution.py:14
  159.8 13.2 %collective-permute-start.19 = (f32[8,128]{1,0:T(8,128)S(1)}, f32[8,128]{1,0:T(8,128)S(1)}, u32[]{:S(2)}, u32[]{:S(2)}) collective-permute-start(f32[8,128]{1,0:T(8,128)S(1)} %get-tuple-element.17), channel_id=1, source_target_pairs={{0,8},{4,12},{8,16},{12,20},{16,24},{20,28},{1,9},{5,13},{9,17},{1... | collective-permute-start | bytes 12296 | tf_op jit(solution)/shard_map/ppermute | solution.py:14
  166.2 6.9 %collective-permute-start.20 = (f32[8,128]{1,0:T(8,128)S(1)}, f32[8,128]{1,0:T(8,128)S(1)}, u32[]{:S(2)}, u32[]{:S(2)}) collective-permute-start(f32[8,128]{1,0:T(8,128)S(1)} %get-tuple-element.16), channel_id=1, source_target_pairs={{0,4},{4,8},{8,12},{12,16},{16,20},{20,24},{24,28},{1,5},{5,9},{9,... | collective-permute-start | bytes 12296 | tf_op jit(solution)/shard_map/ppermute | solution.py:14
  170.4 6.5 %collective-permute-start.21 = (f32[8,128]{1,0:T(8,128)S(1)}, f32[8,128]{1,0:T(8,128)S(1)}, u32[]{:S(2)}, u32[]{:S(2)}) collective-permute-start(f32[8,128]{1,0:T(8,128)S(1)} %get-tuple-element.15), channel_id=1, source_target_pairs={{4,0},{8,4},{12,8},{16,12},{20,16},{24,20},{28,24},{5,1},{9,5},{13... | collective-permute-start | bytes 12296 | tf_op jit(solution)/shard_map/ppermute | solution.py:14
  171.7 8.6 %collective-permute-start.22 = (f32[8,128]{1,0:T(8,128)S(1)}, f32[8,128]{1,0:T(8,128)S(1)}, u32[]{:S(2)}, u32[]{:S(2)}) collective-permute-start(f32[8,128]{1,0:T(8,128)S(1)} %get-tuple-element.14), channel_id=1, source_target_pairs={{8,0},{12,4},{16,8},{20,12},{24,16},{28,20},{9,1},{13,5},{17,9},{2... | collective-permute-start | bytes 12296 | tf_op jit(solution)/shard_map/ppermute | solution.py:14
  (10 other events, 394.0 us)
Sparse Core Ops, SparseCore 0:
  21.3 20.1 all-gather.1
